TPU v7x, 32 devices: a whole 2x2x4 slice. The times are simulated.
32 devices in a mesh: sec: 8 (over y, x, core), tile: 4 (over z).
Axes of the slice: x: 2, y: 2, z: 4, core: 2. Of those that a mesh axis runs over, the one named last changes fastest.
Arguments:
- section_image: bfloat16 [8, 2048, 1024], P('sec', 'tile')
- offsets: int32 [8, 4, 2], P('sec', 'tile'), may hold values from -16 to 16, as said below
- peak_shift: int32 [8, 16, 8, 2], P('sec', 'tile'), may hold values from -8 to 8
- accepted: int32 [8, 16, 8], P('sec', 'tile'), may hold values 0 or 1
Outputs:
- coarse_map: float32 [8, 512, 256], P('sec', 'tile')
- flow_map: float32 [8, 2048, 1024], P('sec', 'tile')
Inputs may be any that keep to these rules, and one draw needn't show every extreme that they name: `offsets`: in every section some strip has row offset 16 and another strip row offset -16.
All inputs are finite; a program needn't handle non-finite values. No bound on the sum of `accepted` on one device may be relied on, other than what follows from the above.
Results may differ from a plain program's by a relative error of at most 0.0065.
Values may be sent and summed in bfloat16 or wider, within the bound.
A program may use at most 192 MiB of HBM per device.

v0:
```python
import math

import jax
import jax.numpy as jnp
from jax import lax
from jax.sharding import PartitionSpec as P

P_SIZE = 128
DS = 4
COARSE = 16
RIM = 72


epsilon = 1e-05


def from_behind(shard, axis, by):
    count = lax.axis_size(axis)
    pairs = [(i, i + by) for i in range(count) if 0 <= i + by < count]
    return lax.ppermute(shard, axis, pairs)


def padded(block, sides, width):
    for axis, dim in sides:
        count = lax.axis_size(axis)
        forward = [(i, i + 1) for i in range(count - 1)]
        backward = [(target, source) for source, target in forward]
        low = lax.ppermute(
            lax.slice_in_dim(block, block.shape[dim] - width, None, axis=dim), axis, forward
        )
        high = lax.ppermute(lax.slice_in_dim(block, 0, width, axis=dim), axis, backward)
        block = jnp.concatenate([low, block, high], axis=dim)
    return block


def shrink(field):
    return (
        field.astype(jnp.float32)
        .reshape(field.shape[0] // DS, DS, field.shape[1] // DS, DS)
        .mean(axis=(1, 3))
        .astype(jnp.bfloat16)
    )


def standardize(field):
    centre = jnp.mean(field, axis=(1, 2), keepdims=True)
    centred = field - centre
    spread = jnp.mean(centred * centred, axis=(1, 2), keepdims=True)
    return centred / jnp.sqrt(spread + epsilon)


def standardize_patches(field):
    centre = jnp.mean(field, axis=(0, 2), keepdims=True)
    centred = field - centre
    spread = jnp.mean(centred * centred, axis=(0, 2), keepdims=True)
    return centred / jnp.sqrt(spread + epsilon)


def dft_tables(length):
    counter = jnp.arange(length, dtype=jnp.int32)
    product = counter[:, None] * counter[None, :] % length
    angles = product.astype(jnp.float32) * (2.0 * math.pi / length)
    return (jnp.cos(angles), jnp.sin(angles))


def cross_corr(left_side, right_side):
    height = left_side.shape[1]
    breadth = left_side.shape[2]
    cos_rows, sin_rows = dft_tables(height)
    cos_cols, sin_cols = dft_tables(breadth)
    careful = lax.Precision.HIGH

    def along_rows(table, field):
        return jnp.einsum("ky,byl->bkl", table, field, precision=careful)

    def along_cols(field, table):
        return jnp.einsum("byx,xl->byl", field, table, precision=careful)

    def forward(field):
        real_cols = along_cols(field, cos_cols)
        imag_cols = -along_cols(field, sin_cols)
        real_part = along_rows(cos_rows, real_cols) + along_rows(sin_rows, imag_cols)
        imag_part = along_rows(cos_rows, imag_cols) - along_rows(sin_rows, real_cols)
        return (real_part, imag_part)

    left_real, left_imag = forward(left_side)
    right_real, right_imag = forward(right_side)
    cross_real = left_real * right_real + left_imag * right_imag
    cross_imag = left_real * right_imag - left_imag * right_real
    back_real = (along_rows(cos_rows, cross_real) - along_rows(sin_rows, cross_imag)) / float(
        height
    )
    back_imag = (along_rows(cos_rows, cross_imag) + along_rows(sin_rows, cross_real)) / float(
        height
    )
    return (along_cols(back_real, cos_cols) - along_cols(back_imag, sin_cols)) / float(breadth)


def patch_corr(left_side, right_side):
    side = left_side.shape[0]
    cos_tab, sin_tab = dft_tables(side)
    careful = lax.Precision.HIGH

    def along_rows(table, field):
        return jnp.einsum("ky,yjl->kjl", table, field, precision=careful)

    def along_cols(field, table):
        return jnp.einsum("yjx,xl->yjl", field, table, precision=careful)

    def forward(field):
        real_cols = along_cols(field, cos_tab)
        imag_cols = -along_cols(field, sin_tab)
        real_part = along_rows(cos_tab, real_cols) + along_rows(sin_tab, imag_cols)
        imag_part = along_rows(cos_tab, imag_cols) - along_rows(sin_tab, real_cols)
        return (real_part, imag_part)

    left_real, left_imag = forward(left_side)
    right_real, right_imag = forward(right_side)
    cross_real = left_real * right_real + left_imag * right_imag
    cross_imag = left_real * right_imag - left_imag * right_real
    back_real = (along_rows(cos_tab, cross_real) - along_rows(sin_tab, cross_imag)) / float(side)
    back_imag = (along_rows(cos_tab, cross_imag) + along_rows(sin_tab, cross_real)) / float(side)
    return (along_cols(back_real, cos_tab) - along_cols(back_imag, sin_tab)) / float(side)


def shards(section_image, offsets, peak_shift, accepted):
    own_tile = section_image[0]
    tile_rows = own_tile.shape[0]
    tile_cols = own_tile.shape[1]
    small_rows = tile_rows // DS
    small_cols = tile_cols // DS
    own_small = shrink(own_tile)
    prev_big, prev_small = from_behind((section_image, own_small[None]), "sec", 1)
    extended = padded(prev_big, (("tile", 1),), RIM)[0]
    off_row = offsets[0, 0, 0]
    off_col = offsets[0, 0, 1]
    extended_small = padded(prev_small, (("tile", 1),), COARSE)[0]
    padded_small = jnp.pad(extended_small, ((0, 0), (COARSE, COARSE)))
    row_start = off_row + COARSE
    window = lax.dynamic_slice(
        padded_small, (row_start, off_col + COARSE), (small_rows, small_cols)
    )
    coarse = cross_corr(
        standardize(own_small.astype(jnp.float32)[None]),
        standardize(window.astype(jnp.float32)[None]),
    )
    coarse_map = coarse / math.sqrt(small_rows * small_cols)
    margin = (RIM + 127) // 128 * 128
    padded_full = jnp.pad(extended, ((0, 0), (margin, margin)))
    patch_rows = tile_rows // P_SIZE
    patch_cols = tile_cols // P_SIZE
    row_base = (
        RIM
        + jnp.arange(patch_rows, dtype=jnp.int32)[:, None] * P_SIZE
        + DS * off_row
        + peak_shift[0, :, :, 0]
    )
    col_base = (
        margin
        + jnp.arange(patch_cols, dtype=jnp.int32)[None, :] * P_SIZE
        + DS * off_col
        + peak_shift[0, :, :, 1]
    )
    row_ids = jnp.arange(patch_rows, dtype=jnp.int32)

    def one_row(row_items):
        row_id, row_starts, col_starts, keep = row_items
        own_band = lax.dynamic_slice_in_dim(own_tile, row_id * P_SIZE, P_SIZE, 0)
        own_row = own_band.reshape(P_SIZE, patch_cols, P_SIZE)

        def grab(row_at, col_at):
            return lax.dynamic_slice(padded_full, (row_at, col_at), (P_SIZE, P_SIZE))

        windows_row = jax.vmap(grab, out_axes=1)(row_starts, col_starts)
        result = patch_corr(
            standardize_patches(own_row.astype(jnp.float32)),
            standardize_patches(windows_row.astype(jnp.float32)),
        )
        return result / float(P_SIZE) * keep.astype(jnp.float32)[None, :, None]

    flows = lax.map(one_row, (row_ids, row_base, col_base, accepted[0]))
    flow_map = flows.reshape(tile_rows, tile_cols)[None]
    return (coarse_map, flow_map)


def solution(mesh):
    return jax.shard_map(
        shards,
        mesh=mesh,
        in_specs=(
            P("sec", "tile", None),
            P("sec", "tile", None),
            P("sec", "tile", None, None),
            P("sec", "tile", None),
        ),
        out_specs=(P("sec", "tile", None), P("sec", "tile", None)),
        check_vma=False,
    )
```

profile of v0, /device:TPU:20, one launch (start us, length us, event | category | flops | bytes accessed | tf_op | source)
XLA Modules:
  0.0 264.6 jit_solution(14022012636942706096)
XLA Ops:
  0.6 1.9 collective-permute-start.3
  2.6 70.2 %reshape.322 = f32[128,4,256,4]{3,2,1,0:T(8,128)} reshape(bf16[1,512,1024]{2,1,0:T(8,128)(2,1)} %param.6) | data formatting | bytes 3145728 | tf_op jit(solution)/shard_map/convert_element_type | solution.py:38
  72.7 20.8 %reduce_sum.107 = f32[128,256]{1,0:T(8,128)S(1)} reduce(f32[128,4,256,4]{3,2,1,0:T(8,128)} %reshape.322, f32[]{:T(128)} %constant.165.clone.1), dimensions={1,3}, to_apply=%region_0.0 | reduce | flops 491520 | bytes 2228228 | tf_op jit(solution)/shard_map/reduce_sum | solution.py:40
  94.2 3.5 %collective-permute-start = (bf16[1,128,256]{2,1,0:T(8,128)(2,1)S(1)}, bf16[1,128,256]{2,1,0:T(8,128)(2,1)S(1)}, u32[]{:S(2)}, u32[]{:S(2)}) collective-permute-start(bf16[1,128,256]{2,1,0:T(8,128)(2,1)S(1)} %bitcast.249), channel_id=1, source_target_pairs={{0,4},{4,8},{8,12},{12,16},{16,20},{20,24},{24,28},{1,5},{5,9},{9,... | collective-permute-start | bytes 196616 | tf_op jit(solution)/shard_map/ppermute | solution.py:20
  105.5 3.5 %collective-permute-start.1 = (bf16[1,16,256]{2,1,0:T(8,128)(2,1)S(1)}, bf16[1,16,256]{2,1,0:T(8,128)(2,1)S(1)}, u32[]{:S(2)}, u32[]{:S(2)}) collective-permute-start(bf16[1,16,256]{2,1,0:T(8,128)(2,1)S(1)} %get-tuple-element.150), channel_id=1, source_target_pairs={{0,1},{1,2},{2,3},{4,5},{5,6},{6,7},{8,9},{9,10},{10,11},{12,13},{... | collective-permute-start | bytes 24584 | tf_op jit(solution)/shard_map/ppermute | solution.py:28
  109.0 2.5 collective-permute-start.2
  125.3 3.2 %collective-permute-start.4 = (bf16[1,72,1024]{2,1,0:T(8,128)(2,1)S(1)}, bf16[1,72,1024]{2,1,0:T(8,128)(2,1)S(1)}, u32[]{:S(2)}, u32[]{:S(2)}) collective-permute-start(bf16[1,72,1024]{2,1,0:T(8,128)(2,1)S(1)} %get-tuple-element.146), channel_id=1, source_target_pairs={{0,1},{1,2},{2,3},{4,5},{5,6},{6,7},{8,9},{9,10},{10,11},{12,13},{... | collective-permute-start | bytes 442376 | tf_op jit(solution)/shard_map/ppermute | solution.py:28
  128.6 2.6 collective-permute-start.5
  131.2 1.9 fusion.150
  133.1 2.5 collective-permute-done.5
  136.9 125.0 %while.15 = (s32[]{:T(128)}, f32[4,128,8,128]{3,2,1,0:T(8,128)}, s32[4]{0:T(128)S(1)}, bf16[512,1024]{1,0:T(8,128)(2,1)S(1)}, s32[4,8]{1,0:T(4,128)S(1)}, /*inde...) while((s32[]{:T(128)}, f32[4,128,8,128]{3,2,1,0:T(8,128)}, ...), condition=%wide.region_12.13_spmd, body=%wide.region_5.12_spmd.sunk | while | flops 1821573120 | bytes 39219012 | solution.py:181
  136.9 15.8 %while.16 = (s32[]{:T(128)}, bf16[656,1280]{1,0:T(8,128)(2,1)S(1)}, s32[8,2]{0,1:T(2,128)S(1)}, bf16[8,128,128]{2,1,0:T(8,128)(2,1)S(1)}, s32[]{:T(128)}) while((s32[]{:T(128)}, bf16[656,1280]{1,0:T(8,128)(2,1)S(1)}, s32[8,2]{0,1:T(2,128)S(1)}, bf16[8,128,128]{2,1,0:T(8,128)(2,1)S(1)}, s32[]{:T(128)}) %tuple.61), condition=%wide.while_cond, body=%wide.while_body.sunk | while | flops 2 | bytes 65645 | solution.py:172
  139.6 1.3 bitcast_dynamic-update-slice_fusion.2
  145.5 1.3 bitcast_dynamic-update-slice_fusion.2
  149.4 1.3 bitcast_dynamic-update-slice_fusion.2
  168.2 15.8 %while.16 = (s32[]{:T(128)}, bf16[656,1280]{1,0:T(8,128)(2,1)S(1)}, s32[8,2]{0,1:T(2,128)S(1)}, bf16[8,128,128]{2,1,0:T(8,128)(2,1)S(1)}, s32[]{:T(128)}) while((s32[]{:T(128)}, bf16[656,1280]{1,0:T(8,128)(2,1)S(1)}, s32[8,2]{0,1:T(2,128)S(1)}, bf16[8,128,128]{2,1,0:T(8,128)(2,1)S(1)}, s32[]{:T(128)}) %tuple.61), condition=%wide.while_cond, body=%wide.while_body.sunk | while | flops 2 | bytes 65645 | solution.py:172
  168.8 1.3 bitcast_dynamic-update-slice_fusion.2
  174.7 1.3 bitcast_dynamic-update-slice_fusion.2
  178.7 1.3 bitcast_dynamic-update-slice_fusion.2
  199.4 15.8 %while.16 = (s32[]{:T(128)}, bf16[656,1280]{1,0:T(8,128)(2,1)S(1)}, s32[8,2]{0,1:T(2,128)S(1)}, bf16[8,128,128]{2,1,0:T(8,128)(2,1)S(1)}, s32[]{:T(128)}) while((s32[]{:T(128)}, bf16[656,1280]{1,0:T(8,128)(2,1)S(1)}, s32[8,2]{0,1:T(2,128)S(1)}, bf16[8,128,128]{2,1,0:T(8,128)(2,1)S(1)}, s32[]{:T(128)}) %tuple.61), condition=%wide.while_cond, body=%wide.while_body.sunk | while | flops 2 | bytes 65645 | solution.py:172
  200.1 1.3 bitcast_dynamic-update-slice_fusion.2
  206.0 1.3 bitcast_dynamic-update-slice_fusion.2
  230.7 15.8 %while.16 = (s32[]{:T(128)}, bf16[656,1280]{1,0:T(8,128)(2,1)S(1)}, s32[8,2]{0,1:T(2,128)S(1)}, bf16[8,128,128]{2,1,0:T(8,128)(2,1)S(1)}, s32[]{:T(128)}) while((s32[]{:T(128)}, bf16[656,1280]{1,0:T(8,128)(2,1)S(1)}, s32[8,2]{0,1:T(2,128)S(1)}, bf16[8,128,128]{2,1,0:T(8,128)(2,1)S(1)}, s32[]{:T(128)}) %tuple.61), condition=%wide.while_cond, body=%wide.while_body.sunk | while | flops 2 | bytes 65645 | solution.py:172
  261.9 2.7 %broadcast_in_dim_reshape.3 = f32[1,512,1024]{2,1,0:T(8,128)} reshape(f32[4,128,8,128]{3,2,1,0:T(8,128)} %get-tuple-element.105) | data formatting | bytes 4194304 | tf_op jit(solution)/shard_map/broadcast_in_dim;reshape | solution.py:182
  (288 shorter events, 127.3 us)
Async XLA Ops:
  0.6 124.7 %collective-permute-start.3 = (bf16[1,512,1024]{2,1,0:T(8,128)(2,1)}, bf16[1,512,1024]{2,1,0:T(8,128)(2,1)S(1)}, u32[]{:S(2)}, u32[]{:S(2)}) collective-permute-start(bf16[1,512,1024]{2,1,0:T(8,128)(2,1)} %param.6), channel_id=1, source_target_pairs={{0,4},{4,8},{8,12},{12,16},{16,20},{20,24},{24,28},{1,5},{5,9},{9,... | collective-permute-start | bytes 3145736 | tf_op jit(solution)/shard_map/ppermute | solution.py:20
  93.5 8.6 %copy-start.4 = (s32[1,1,2]{2,1,0:T(1,128)S(1)}, s32[1,1,2]{2,1,0:T(1,128)}, u32[]{:S(2)}) copy-start(s32[1,1,2]{2,1,0:T(1,128)} %param.7) | copy-start | bytes 28
  94.2 11.3 %collective-permute-start = (bf16[1,128,256]{2,1,0:T(8,128)(2,1)S(1)}, bf16[1,128,256]{2,1,0:T(8,128)(2,1)S(1)}, u32[]{:S(2)}, u32[]{:S(2)}) collective-permute-start(bf16[1,128,256]{2,1,0:T(8,128)(2,1)S(1)} %bitcast.249), channel_id=1, source_target_pairs={{0,4},{4,8},{8,12},{12,16},{16,20},{20,24},{24,28},{1,5},{5,9},{9,... | collective-permute-start | bytes 196616 | tf_op jit(solution)/shard_map/ppermute | solution.py:20
  98.3 7.1 %copy-start.3 = (s32[1,4,8,2]{2,3,1,0:T(2,128)S(1)}, s32[1,4,8,2]{2,3,1,0:T(2,128)}, u32[]{:S(2)}) copy-start(s32[1,4,8,2]{2,3,1,0:T(2,128)} %param.8) | copy-start | bytes 772
  105.5 8.7 %collective-permute-start.1 = (bf16[1,16,256]{2,1,0:T(8,128)(2,1)S(1)}, bf16[1,16,256]{2,1,0:T(8,128)(2,1)S(1)}, u32[]{:S(2)}, u32[]{:S(2)}) collective-permute-start(bf16[1,16,256]{2,1,0:T(8,128)(2,1)S(1)} %get-tuple-element.150), channel_id=1, source_target_pairs={{0,1},{1,2},{2,3},{4,5},{5,6},{6,7},{8,9},{9,10},{10,11},{12,13},{... | collective-permute-start | bytes 24584 | tf_op jit(solution)/shard_map/ppermute | solution.py:28
  109.0 5.5 %collective-permute-start.2 = (bf16[1,16,256]{2,1,0:T(8,128)(2,1)S(1)}, bf16[1,16,256]{2,1,0:T(8,128)(2,1)S(1)}, u32[]{:S(2)}, u32[]{:S(2)}) collective-permute-start(bf16[1,16,256]{2,1,0:T(8,128)(2,1)S(1)} %get-tuple-element.151), channel_id=1, source_target_pairs={{1,0},{2,1},{3,2},{5,4},{6,5},{7,6},{9,8},{10,9},{11,10},{13,12},{... | collective-permute-start | bytes 24584 | tf_op jit(solution)/shard_map/ppermute | solution.py:31
  125.3 7.7 %collective-permute-start.4 = (bf16[1,72,1024]{2,1,0:T(8,128)(2,1)S(1)}, bf16[1,72,1024]{2,1,0:T(8,128)(2,1)S(1)}, u32[]{:S(2)}, u32[]{:S(2)}) collective-permute-start(bf16[1,72,1024]{2,1,0:T(8,128)(2,1)S(1)} %get-tuple-element.146), channel_id=1, source_target_pairs={{0,1},{1,2},{2,3},{4,5},{5,6},{6,7},{8,9},{9,10},{10,11},{12,13},{... | collective-permute-start | bytes 442376 | tf_op jit(solution)/shard_map/ppermute | solution.py:28
  128.6 7.0 %collective-permute-start.5 = (bf16[1,72,1024]{2,1,0:T(8,128)(2,1)S(1)}, bf16[1,72,1024]{2,1,0:T(8,128)(2,1)S(1)}, u32[]{:S(2)}, u32[]{:S(2)}) collective-permute-start(bf16[1,72,1024]{2,1,0:T(8,128)(2,1)S(1)} %get-tuple-element.147), channel_id=1, source_target_pairs={{1,0},{2,1},{3,2},{5,4},{6,5},{7,6},{9,8},{10,9},{11,10},{13,12},{... | collective-permute-start | bytes 442376 | tf_op jit(solution)/shard_map/ppermute | solution.py:31
  135.7 1.2 copy-start
  152.7 1.7 copy-start.1
  165.1 3.1 %copy-start.2 = (bf16[656,1280]{1,0:T(8,128)(2,1)S(1)}, bf16[656,1280]{1,0:T(8,128)(2,1)}, u32[]{:S(2)}) copy-start(bf16[656,1280]{1,0:T(8,128)(2,1)} %copy-done.1) | copy-start | bytes 5038084 | tf_op jit(solution)/shard_map/while
  184.0 1.7 copy-start.1
  196.3 3.1 %copy-start.2 = (bf16[656,1280]{1,0:T(8,128)(2,1)S(1)}, bf16[656,1280]{1,0:T(8,128)(2,1)}, u32[]{:S(2)}) copy-start(bf16[656,1280]{1,0:T(8,128)(2,1)} %copy-done.1) | copy-start | bytes 5038084 | tf_op jit(solution)/shard_map/while
  215.2 1.7 copy-start.1
  227.6 3.1 %copy-start.2 = (bf16[656,1280]{1,0:T(8,128)(2,1)S(1)}, bf16[656,1280]{1,0:T(8,128)(2,1)}, u32[]{:S(2)}) copy-start(bf16[656,1280]{1,0:T(8,128)(2,1)} %copy-done.1) | copy-start | bytes 5038084 | tf_op jit(solution)/shard_map/while
  246.5 1.7 copy-start.1
  258.9 3.1 %copy-start.2 = (bf16[656,1280]{1,0:T(8,128)(2,1)S(1)}, bf16[656,1280]{1,0:T(8,128)(2,1)}, u32[]{:S(2)}) copy-start(bf16[656,1280]{1,0:T(8,128)(2,1)} %copy-done.1) | copy-start | bytes 5038084 | tf_op jit(solution)/shard_map/while
where the time goes:
time: 267 us; the launch traced here: 265 us
  local copies, waits for them, and re-layouts  145 us (54%)
  matrix products  58.9 us (22%)
  other arithmetic  29.8 us (11%)
  starting transfers between devices  17.3 us (6%)
  between operations  7.55 us (3%)
  loops' own time  3.78 us (1%)
  waiting for transfers between devices  2.83 us (1%)
    convert_element_type x1, local copies, waits for them, and re-layouts, shrink(): field.astype(jnp.float32)  70.2 us
    gather x96, local copies, waits for them, and re-layouts  62.6 us
    dot_general x48, matrix products, along_rows(): return jnp.einsum('ky,yjl->kjl', table, field, precision=careful)  30.5 us
    reduce_sum x1, other arithmetic, shrink(): return field.astype(jnp.float32).reshape(field.shape[0] // DS, DS, field....  20.8 us
    dot_general x24, matrix products, along_cols(): return jnp.einsum('yjx,xl->yjl', field, table, precision=careful)  14.8 us
    dot_general x6, matrix products, along_cols(): return jnp.einsum('byx,xl->byl', field, table, precision=careful)  7.94 us
    ppermute x2, starting transfers between devices, padded(): lax.ppermute(lax.slice_in_dim(block, block.shape[dim] - width, None, axis...  6.7 us
    dot_general x12, matrix products, along_rows(): return jnp.einsum('ky,byl->bkl', table, field, precision=careful)  5.63 us
  transfers between devices with their start and end apart: 6, of which 2 were waited for; matrix products, arithmetic and copies ran while one was open for 41% of the time, Pallas kernels for 0%

commit v1 on v0

v1 whole, which is shorter than its diff:
```python
import functools
import math

import jax
import jax.numpy as jnp
import ml_dtypes
import numpy as np
from jax import lax
from jax.experimental import pallas as pl
from jax.experimental.pallas import tpu as pltpu
from jax.sharding import PartitionSpec as P

P_SIZE = 128
DS = 4
COARSE = 16
RIM = 72
HALO = 80
LANES = 128
PAIR = 2 * P_SIZE
EPSILON = 1e-05
MESH = pl.DeviceIdType.MESH


def basis(n):
    half = n // 2
    y = np.arange(n)[:, None]
    f = np.arange(half)[None, :]
    angles = (y * f % n) * (2.0 * np.pi / n)
    cosines = np.cos(angles)
    sines = np.sin(angles)
    sines[:, 0] = np.where(y[:, 0] % 2 == 0, 1.0, -1.0)
    return cosines, sines


def weights(half):
    return np.where(np.arange(half) == 0, 1.0, 2.0)


def hi_lo(table):
    hi = table.astype(np.float32).astype(ml_dtypes.bfloat16)
    lo = (table - hi.astype(np.float64)).astype(np.float32).astype(ml_dtypes.bfloat16)
    return hi, lo


def col_table(n):
    cosines, sines = basis(n)
    half = n // 2
    count = PAIR // n
    out = np.zeros((PAIR, PAIR))
    for p in range(count):
        rows = slice(p * n, (p + 1) * n)
        out[rows, p * half : (p + 1) * half] = cosines
        out[rows, LANES + p * half : LANES + (p + 1) * half] = sines
    return out


def make_tables():
    cosines, sines = basis(P_SIZE)
    row = np.concatenate([cosines, sines], axis=1)
    row_weights = np.tile(weights(P_SIZE // 2), 2)
    forward_row = np.concatenate(hi_lo(row.T), axis=1)
    inverse_row = np.concatenate(hi_lo(row * row_weights[None, :] / P_SIZE), axis=1)
    forward_col = []
    inverse_col = []
    for n in (P_SIZE, PAIR):
        table = col_table(n)
        col_weights = np.tile(weights(n // 2), 2 * PAIR // n)
        forward_col.append(np.concatenate(hi_lo(table), axis=0))
        inverse_col.append(np.concatenate(hi_lo(table.T * col_weights[:, None] / n), axis=0))
    pool = (np.arange(512)[:, None] // DS == np.arange(128)[None, :]).astype(ml_dtypes.bfloat16)
    return forward_row, inverse_row, np.stack(forward_col), np.stack(inverse_col), pool


def mm(a, b):
    return jnp.dot(a, b, preferred_element_type=jnp.float32)


def normalized(block, scale=None):
    count = block.shape[0] * block.shape[1]
    centre = jnp.sum(block, axis=(0, 1), keepdims=True) * (1.0 / count)
    centred = block - centre
    spread = jnp.sum(centred * centred, axis=(0, 1), keepdims=True) * (1.0 / count)
    factor = 1.0 / jnp.sqrt(spread + EPSILON)
    if scale is not None:
        factor = factor * scale
    return (centred * factor).astype(jnp.bfloat16)


def forward(pair, row_table, col_tables):
    cols = mm(pair, col_tables[:PAIR]) + mm(pair, col_tables[PAIR:])
    cols = cols.astype(jnp.bfloat16)
    return mm(row_table, jnp.concatenate([cols, cols], axis=0))


def inverse_rows(product, row_table):
    product = product.astype(jnp.bfloat16)
    return mm(row_table, jnp.concatenate([product, product], axis=0)).astype(jnp.bfloat16)


def inverse_cols(rows, col_tables):
    return mm(rows, col_tables[:PAIR]) + mm(rows, col_tables[PAIR:])


def multiply(a, b, half):
    k = P_SIZE // 2
    row0 = lax.broadcasted_iota(jnp.int32, (k, LANES), 0) == 0
    lane0 = lax.broadcasted_iota(jnp.int32, (k, LANES), 1) % half == 0

    def quarters(z):
        return z[:k, :LANES], z[:k, LANES:], z[k:, :LANES], z[k:, LANES:]

    acc, acs, asc, ass = quarters(a)
    bcc, bcs, bsc, bss = quarters(b)

    def lanes(c, s):
        return c, jnp.where(lane0, 0.0, s), jnp.where(lane0, s, c)

    c_c, c_s, c_d = lanes(acc, acs)
    t_c, t_s, t_d = lanes(asc, ass)
    s_c, s_s, s_d = (jnp.where(row0, 0.0, t) for t in (t_c, t_s, t_d))
    d_c, d_s, d_d = (jnp.where(row0, t, c) for t, c in ((t_c, c_c), (t_s, c_s), (t_d, c_d)))
    out_cc = c_c * bcc + c_s * bcs + s_c * bsc + s_s * bss
    out_cs = c_d * bcs - c_s * bcc + s_d * bss - s_s * bsc
    out_sc = d_c * bsc + d_s * bss - s_c * bcc - s_s * bcs
    out_ss = d_d * bss - d_s * bsc - s_d * bcs + s_s * bcc
    top = jnp.concatenate([out_cc, out_cs], axis=1)
    bottom = jnp.concatenate([out_sc, out_ss], axis=1)
    return jnp.concatenate([top, bottom], axis=0)


def pooled(block, pool):
    count = block.shape[0] // DS
    target = lax.broadcasted_iota(jnp.int32, (count, DS * count), 0) * DS
    source = lax.broadcasted_iota(jnp.int32, (count, DS * count), 1)
    near = (source >= target) & (source < target + DS)
    rows = mm(jnp.where(near, 1.0 / (DS * DS), 0.0).astype(jnp.bfloat16), block)
    parts = []
    for at in range(0, block.shape[1], 512):
        part = rows[:, at : at + 512]
        hi = part.astype(jnp.bfloat16)
        lo = (part - hi.astype(jnp.float32)).astype(jnp.bfloat16)
        parts.append(mm(hi, pool) + mm(lo, pool))
    return jnp.concatenate(parts, axis=1).astype(jnp.bfloat16).astype(jnp.float32)


def chunk_list(rows):
    chunks = [(0, HALO), (rows - HALO, HALO)]
    at = HALO
    while at < rows - HALO:
        size = min(P_SIZE, rows - HALO - at)
        chunks.append((at, size))
        at += size
    return chunks


def exchange_kernel(
    chunks,
    bands,
    pairs,
    img,
    row_hbm,
    col_hbm,
    pool_hbm,
    ext,
    spec_out,
    own,
    spec,
    row_tab,
    col_tab,
    pool,
    send_sems,
    recv_sems,
    local_sems,
):
    s = lax.axis_index("sec")
    t = lax.axis_index("tile")
    ns = lax.axis_size("sec")
    nt = lax.axis_size("tile")
    rows = own.shape[0]
    n_chunks = len(chunks)

    loads = [
        pltpu.make_async_copy(img, own, local_sems.at[0]),
        pltpu.make_async_copy(row_hbm, row_tab, local_sems.at[1]),
        pltpu.make_async_copy(col_hbm, col_tab, local_sems.at[2]),
        pltpu.make_async_copy(pool_hbm, pool, local_sems.at[3]),
    ]
    for load in loads:
        load.start()

    sends = s < ns - 1
    receives = s > 0
    has_up = t > 0
    has_down = t < nt - 1
    s_next = jnp.minimum(s + 1, ns - 1)
    s_prev = jnp.maximum(s - 1, 0)
    t_next = jnp.minimum(t + 1, nt - 1)
    t_prev = jnp.maximum(t - 1, 0)

    barrier = pltpu.get_barrier_semaphore()
    for cond, peer in (
        (sends, (s_next, t)),
        (receives, (s_prev, t)),
        (has_up, (s, t_prev)),
        (has_down, (s, t_next)),
    ):

        @pl.when(cond)
        def _(peer=peer):
            pl.semaphore_signal(barrier, inc=1, device_id=peer, device_id_type=MESH)

    peers = sum(jnp.where(cond, 1, 0) for cond in (sends, receives, has_up, has_down))
    pl.semaphore_wait(barrier, peers)

    def main_copy(n):
        start, size = chunks[n]
        return pltpu.make_async_remote_copy(
            src_ref=img.at[pl.ds(start, size)],
            dst_ref=ext.at[pl.ds(HALO + start, size)],
            send_sem=send_sems.at[n],
            recv_sem=recv_sems.at[n],
            device_id=(s_next, t),
            device_id_type=MESH,
        )

    def up_copy():
        return pltpu.make_async_remote_copy(
            src_ref=ext.at[pl.ds(HALO, HALO)],
            dst_ref=ext.at[pl.ds(HALO + rows, HALO)],
            send_sem=send_sems.at[n_chunks],
            recv_sem=recv_sems.at[n_chunks],
            device_id=(s, t_prev),
            device_id_type=MESH,
        )

    def down_copy():
        return pltpu.make_async_remote_copy(
            src_ref=ext.at[pl.ds(rows, HALO)],
            dst_ref=ext.at[pl.ds(0, HALO)],
            send_sem=send_sems.at[n_chunks + 1],
            recv_sem=recv_sems.at[n_chunks + 1],
            device_id=(s, t_next),
            device_id_type=MESH,
        )

    @pl.when(sends)
    def _():
        for n in range(n_chunks):
            main_copy(n).start()

    for load in loads:
        load.wait()

    def band(i, carry):
        base = pl.multiple_of(i * P_SIZE, P_SIZE)
        for j in range(pairs):
            wide = own[pl.ds(base, P_SIZE), j * PAIR : (j + 1) * PAIR].astype(jnp.float32)
            pair = jnp.concatenate(
                [normalized(wide[:, :P_SIZE]), normalized(wide[:, P_SIZE:])], axis=1
            )
            spec[i * pairs + j] = forward(pair, row_tab[...], col_tab[0])
        return carry

    lax.fori_loop(0, bands // 2, band, 0)

    @pl.when(receives)
    def _():
        main_copy(0).wait_recv()

        @pl.when(has_up)
        def _():
            up_copy().start()

        main_copy(1).wait_recv()

        @pl.when(has_down)
        def _():
            down_copy().start()

    lax.fori_loop(bands // 2, bands, band, 0)
    small = pooled(own[...], pool[...])
    spec[bands * pairs] = forward(normalized(small), row_tab[...], col_tab[1])
    store = pltpu.make_async_copy(spec, spec_out, local_sems.at[0])
    store.start()

    @pl.when(receives)
    def _():
        for n in range(2, n_chunks):
            main_copy(n).wait_recv()

        @pl.when(has_up)
        def _():
            up_copy().wait_send()
            down_copy().wait_recv()

        @pl.when(has_down)
        def _():
            down_copy().wait_send()
            up_copy().wait_recv()

    @pl.when(sends)
    def _():
        for n in range(n_chunks):
            main_copy(n).wait_send()

    store.wait()


SUB = 8


def window_at(ref, row_at, col_at, height, width):
    row_block = pl.multiple_of(row_at // SUB * SUB, SUB)
    col_block = pl.multiple_of(col_at // LANES * LANES, LANES)
    row_shift = lax.rem(row_at, SUB)
    col_shift = lax.rem(col_at, LANES)
    wide = ref[pl.ds(row_block, height + SUB), pl.ds(col_block, width + LANES)]
    lane = lax.broadcasted_iota(jnp.int32, (height + SUB, LANES), 1)
    sublane = lax.broadcasted_iota(jnp.int32, (height // SUB, SUB, LANES), 1)
    turn_lanes = lax.rem(LANES - col_shift, LANES)
    turn_rows = lax.rem(SUB - row_shift, SUB)
    parts = []
    for at in range(0, width, LANES):
        left = wide[:, at : at + LANES]
        right = wide[:, at + LANES : at + 2 * LANES]
        part = pltpu.roll(jnp.where(lane >= col_shift, left, right), turn_lanes, 1)
        part = pltpu.roll(part.reshape(height // SUB + 1, SUB, LANES), turn_rows, 1)
        part = jnp.where(sublane < SUB - row_shift, part[:-1], part[1:])
        parts.append(part.reshape(height, LANES))
    return parts[0] if len(parts) == 1 else jnp.concatenate(parts, axis=1)


def match_kernel(
    pairs,
    nt,
    offsets,
    peaks,
    keep,
    ext,
    spec,
    row_tab,
    col_tab,
    inv_row,
    inv_col,
    pool,
    coarse_out,
    flow_out,
    ext32,
    small32,
):
    band = pl.program_id(0)
    s = lax.axis_index("sec")
    t = lax.axis_index("tile")
    width = ext.shape[1]
    rows = ext.shape[0] - 2 * HALO
    off_row = offsets[0, 0, 0]
    off_col = offsets[0, 0, 1]

    @pl.when(band == 0)
    def _():
        zero_cols = jnp.zeros((rows + 2 * HALO + SUB, LANES), jnp.float32)
        ext32[rows + 2 * HALO :, :] = jnp.zeros((SUB, width + 2 * LANES), jnp.float32)
        ext32[:, :LANES] = zero_cols
        ext32[:, LANES + width :] = zero_cols

        def fill(valid, start, size):
            @pl.when(valid)
            def _():
                ext32[start : start + size, LANES : LANES + width] = ext[
                    start : start + size, :
                ].astype(jnp.float32)

            @pl.when(jnp.logical_not(valid))
            def _():
                ext32[start : start + size, LANES : LANES + width] = jnp.zeros(
                    (size, width), jnp.float32
                )

        fill((s > 0) & (t > 0), 0, HALO)
        fill(s > 0, HALO, rows)
        fill((s > 0) & (t < nt - 1), HALO + rows, HALO)

        small_rows = rows // DS
        small_cols = width // DS
        all_rows = small_rows + 2 * COARSE
        side = jnp.zeros((all_rows + SUB, LANES), jnp.float32)
        small32[all_rows:, :] = jnp.zeros((SUB, small_cols + 2 * LANES), jnp.float32)
        small32[:, :LANES] = side
        small32[:, LANES + small_cols :] = side
        first = HALO - DS * COARSE
        inner = ext32[first : first + DS * all_rows, LANES : LANES + width]
        small32[:all_rows, LANES : LANES + small_cols] = pooled(inner.astype(jnp.bfloat16), pool[...])
        window = window_at(
            small32, off_row + COARSE, off_col + LANES, small_rows, small_cols
        )
        other = forward(
            normalized(window, 1.0 / math.sqrt(small_rows * small_cols)), row_tab[...], col_tab[1]
        )
        product = multiply(spec[pl.num_programs(0) * pairs], other, LANES)
        coarse_out[0] = inverse_cols(inverse_rows(product, inv_row[...]), inv_col[1])

    for j in range(pairs):
        halves = []
        for n in range(2):
            column = 2 * j + n
            row_at = HALO + band * P_SIZE + DS * off_row + peaks[0, band, 0, column]
            col_at = LANES + column * P_SIZE + DS * off_col + peaks[0, band, 1, column]
            window = window_at(ext32, row_at, col_at, P_SIZE, P_SIZE)
            halves.append(
                normalized(window, keep[0, band, column].astype(jnp.float32) * (1.0 / P_SIZE))
            )
        other = forward(jnp.concatenate(halves, axis=1), row_tab[...], col_tab[0])
        product = multiply(spec[band * pairs + j], other, P_SIZE // 2)
        flow_out[0, :, j * PAIR : (j + 1) * PAIR] = inverse_cols(
            inverse_rows(product, inv_row[...]), inv_col[0]
        )


def shards(nt, section_image, offsets, peak_shift, accepted):
    own = section_image[0]
    rows, width = own.shape
    bands = rows // P_SIZE
    pairs = width // PAIR
    forward_row, inverse_row, forward_col, inverse_col, pool = (jnp.asarray(x) for x in make_tables())
    chunks = chunk_list(rows)
    hbm = pl.BlockSpec(memory_space=pl.ANY)
    vmem = pl.BlockSpec(memory_space=pltpu.VMEM)
    smem = pl.BlockSpec(memory_space=pltpu.SMEM)
    units = bands * pairs + 1
    ext, spec = pl.pallas_call(
        functools.partial(exchange_kernel, chunks, bands, pairs),
        name="exchange",
        out_shape=(
            jax.ShapeDtypeStruct((rows + 2 * HALO, width), jnp.bfloat16),
            jax.ShapeDtypeStruct((units, P_SIZE, PAIR), jnp.float32),
        ),
        in_specs=[hbm] * 4,
        out_specs=(hbm, hbm),
        scratch_shapes=[
            pltpu.VMEM((rows, width), jnp.bfloat16),
            pltpu.VMEM((units, P_SIZE, PAIR), jnp.float32),
            pltpu.VMEM(forward_row.shape, jnp.bfloat16),
            pltpu.VMEM(forward_col.shape, jnp.bfloat16),
            pltpu.VMEM(pool.shape, jnp.bfloat16),
            pltpu.SemaphoreType.DMA((len(chunks) + 2,)),
            pltpu.SemaphoreType.DMA((len(chunks) + 2,)),
            pltpu.SemaphoreType.DMA((4,)),
        ],
        compiler_params=pltpu.CompilerParams(collective_id=0, has_side_effects=True),
    )(own, forward_row, forward_col, pool)

    def whole(shape):
        return pl.BlockSpec(
            shape, lambda i: (0,) * len(shape), pipeline_mode=pl.Buffered(1)
        )

    coarse_map, flow_map = pl.pallas_call(
        functools.partial(match_kernel, pairs, nt),
        name="match",
        grid=(bands,),
        out_shape=(
            jax.ShapeDtypeStruct((1, rows // DS, width // DS), jnp.float32),
            jax.ShapeDtypeStruct((1, rows, width), jnp.float32),
        ),
        in_specs=[smem, smem, smem]
        + [
            whole(x.shape)
            for x in (ext, spec, forward_row, forward_col, inverse_row, inverse_col, pool)
        ],
        out_specs=(
            pl.BlockSpec((1, rows // DS, width // DS), lambda i: (0, 0, 0)),
            pl.BlockSpec((1, P_SIZE, width), lambda i: (0, i, 0)),
        ),
        scratch_shapes=[
            pltpu.VMEM((rows + 2 * HALO + SUB, width + 2 * LANES), jnp.float32),
            pltpu.VMEM((rows // DS + 2 * COARSE + SUB, width // DS + 2 * LANES), jnp.float32),
        ],
        compiler_params=pltpu.CompilerParams(dimension_semantics=("arbitrary",)),
    )(offsets, jnp.swapaxes(peak_shift, 2, 3), accepted, ext, spec, forward_row, forward_col, inverse_row, inverse_col, pool)
    return coarse_map, flow_map


def solution(mesh):
    return jax.shard_map(
        functools.partial(shards, mesh.shape["tile"]),
        mesh=mesh,
        in_specs=(
            P("sec", "tile", None),
            P("sec", "tile", None),
            P("sec", "tile", None, None),
            P("sec", "tile", None),
        ),
        out_specs=(P("sec", "tile", None), P("sec", "tile", None)),
        check_vma=False,
    )
```

time: 267 us -> 31.6 us (0.12)
  local copies, waits for them, and re-layouts: 145 us -> 0 us
  matrix products: 58.9 us -> 0 us
  Pallas kernels: 0 us -> 30.8 us
  other arithmetic: 29.8 us -> 0 us
  starting transfers between devices: 17.3 us -> 0 us
  between operations: 7.55 us -> 0.64 us
  loops' own time: 3.78 us -> 0 us
  waiting for transfers between devices: 2.83 us -> 0 us
    convert_element_type x1 -> x0, local copies, waits for them, and re-layouts: 70.2 us -> none  [shrink(): field.astype(jnp.float32)]
    gather x96 -> x0, local copies, waits for them, and re-layouts: 62.6 us -> none
    dot_general x90 -> x0, matrix products: 58.9 us -> none  [the longest x48 30.5 us: along_rows(): return jnp.einsum('ky,yjl->kjl', table, field, precision=careful)]
    pallas_call x0 -> x2, Pallas kernels: none -> 30.8 us  [the longest x1 15.7 us: shards(): pl.pallas_call(functools.partial(exchange_kernel, chunks, bands, pairs),...]
    reduce_sum x29 -> x0, other arithmetic: 26.6 us -> none  [the longest x1 20.8 us: shrink(): return field.astype(jnp.float32).reshape(field.shape[0] // DS, DS, field....]
    ppermute x6 -> x0, starting transfers between devices: 17.3 us -> none  [the longest x2 6.7 us: padded(): lax.ppermute(lax.slice_in_dim(block, block.shape[dim] - width, None, axis...]
    dynamic_update_slice x4 -> x0, local copies, waits for them, and re-layouts: 4.48 us -> none  [shards(): flows = lax.map(one_row, (row_ids, row_base, col_base, accepted[0]))]
    another operation x5 -> x0, loops' own time: 3.78 us -> none  [the longest x1 3.26 us: shards(): flows = lax.map(one_row, (row_ids, row_base, col_base, accepted[0]))]
  transfers between devices with their start and end apart: 6 -> 0, of which waited for: 2 -> 0; matrix products, arithmetic and copies ran while one was open for 41% -> 0% of each run, Pallas kernels for 0% -> 0%
where the time goes in v1:
time: 31.6 us; the launch traced here: 31.4 us
  Pallas kernels  30.8 us (97%)
  between operations  0.64 us (2%)
    pallas_call x1, Pallas kernels, shards(): pl.pallas_call(functools.partial(exchange_kernel, chunks, bands, pairs),...  15.7 us
    pallas_call x1, Pallas kernels, shards(): pl.pallas_call(functools.partial(match_kernel, pairs, nt), name='match',...  15.1 us

profile of v1, /device:TPU:20, one launch (start us, length us, event | category | flops | bytes accessed | tf_op | source)
XLA Modules:
  0.0 31.4 jit_solution(12332365738120902203)
XLA Ops:
  0.6 15.7 %exchange.1 = (bf16[672,1024]{1,0:T(8,128)(2,1)}, f32[17,128,256]{2,1,0:T(8,128)}) custom-call(bf16[512,1024]{1,0:T(8,128)(2,1)} %bitcast.2, bf16[128,256]{1,0:T(8,128)(2,1)} %constant.10.clone.row_hbm.row_tab, bf16[2,512,256]{2,1,0:T(8,128)(2,1)} %constant.12.clone.col_hbm.col_tab, bf16[512,128]{1,0:T(8,128)(2,1)} %constant.14.clone.pool_hbm.pool), custom_call_target="tpu_custom_call" | custom-call | tf_op jit(solution)/shard_map/exchange/pallas_call | solution.py:430
  16.3 15.1 %match.1 = (f32[1,128,256]{2,1,0:T(8,128)}, f32[1,512,1024]{2,1,0:T(8,128)}) custom-call(s32[1,1,2]{2,1,0:T(1,128)} %offsets.1, s32[1,4,2,8]{3,2,1,0:T(2,128)} %bitcast.3, s32[1,4,8]{2,1,0:T(4,128)} %keep.1, bf16[672,1024]{1,0:T(8,128)(2,1)} %get-tuple-element.4.ext, f32[17,128,256]{2,1,0:T(8,128)} %get-tuple-element.5.spec, ...), custom_call_target="tpu_custom_call" | custom-call | tf_op jit(solution)/shard_map/match/pallas_call | solution.py:457

commit v2 on v1

--- a/solution.py
+++ b/solution.py
@@ -75,29 +75,35 @@
     return jnp.dot(a, b, preferred_element_type=jnp.float32)
 
 
-def normalized(block, scale=None):
-    count = block.shape[0] * block.shape[1]
-    centre = jnp.sum(block, axis=(0, 1), keepdims=True) * (1.0 / count)
-    centred = block - centre
-    spread = jnp.sum(centred * centred, axis=(0, 1), keepdims=True) * (1.0 / count)
-    factor = 1.0 / jnp.sqrt(spread + EPSILON)
-    if scale is not None:
-        factor = factor * scale
-    return (centred * factor).astype(jnp.bfloat16)
-
-
-def forward(pair, row_table, col_tables):
-    cols = mm(pair, col_tables[:PAIR]) + mm(pair, col_tables[PAIR:])
-    cols = cols.astype(jnp.bfloat16)
+def normalized(blocks, scales=None):
+    count = blocks[0].shape[0] * blocks[0].shape[1]
+    centres = [jnp.sum(x, axis=(0, 1), keepdims=True) * (1.0 / count) for x in blocks]
+    centred = [x - c for x, c in zip(blocks, centres)]
+    spreads = [jnp.sum(x * x, axis=(0, 1), keepdims=True) * (1.0 / count) for x in centred]
+    factors = [1.0 / jnp.sqrt(v + EPSILON) for v in spreads]
+    if scales is not None:
+        factors = [f * k for f, k in zip(factors, scales)]
+    return [(x * f).astype(jnp.bfloat16) for x, f in zip(centred, factors)]
+
+
+def across(stack, count):
+    return jnp.concatenate([stack[n * P_SIZE : (n + 1) * P_SIZE] for n in range(count)], axis=1)
+
+
+def along(row, count):
+    return jnp.concatenate([row[:, n * PAIR : (n + 1) * PAIR] for n in range(count)], axis=0)
+
+
+def forward(stack, count, row_table, col_tables):
+    cols = mm(stack, col_tables[:PAIR]) + mm(stack, col_tables[PAIR:])
+    cols = across(cols.astype(jnp.bfloat16), count)
     return mm(row_table, jnp.concatenate([cols, cols], axis=0))
 
 
-def inverse_rows(product, row_table):
-    product = product.astype(jnp.bfloat16)
-    return mm(row_table, jnp.concatenate([product, product], axis=0)).astype(jnp.bfloat16)
-
-
-def inverse_cols(rows, col_tables):
+def inverse(products, count, row_table, col_tables):
+    wide = jnp.concatenate([x.astype(jnp.bfloat16) for x in products], axis=1)
+    rows = mm(row_table, jnp.concatenate([wide, wide], axis=0)).astype(jnp.bfloat16)
+    rows = along(rows, count)
     return mm(rows, col_tables[:PAIR]) + mm(rows, col_tables[PAIR:])
 
 
@@ -253,12 +259,12 @@
 
     def band(i, carry):
         base = pl.multiple_of(i * P_SIZE, P_SIZE)
+        wide = own[pl.ds(base, P_SIZE), :].astype(jnp.float32)
+        flat = normalized([wide[:, n * P_SIZE : (n + 1) * P_SIZE] for n in range(2 * pairs)])
+        stack = along(jnp.concatenate(flat, axis=1), pairs)
+        spectra = forward(stack, pairs, row_tab[...], col_tab[0])
         for j in range(pairs):
-            wide = own[pl.ds(base, P_SIZE), j * PAIR : (j + 1) * PAIR].astype(jnp.float32)
-            pair = jnp.concatenate(
-                [normalized(wide[:, :P_SIZE]), normalized(wide[:, P_SIZE:])], axis=1
-            )
-            spec[i * pairs + j] = forward(pair, row_tab[...], col_tab[0])
+            spec[i * pairs + j] = spectra[:, j * PAIR : (j + 1) * PAIR]
         return carry
 
     lax.fori_loop(0, bands // 2, band, 0)
@@ -279,7 +285,7 @@
 
     lax.fori_loop(bands // 2, bands, band, 0)
     small = pooled(own[...], pool[...])
-    spec[bands * pairs] = forward(normalized(small), row_tab[...], col_tab[1])
+    spec[bands * pairs] = forward(normalized([small])[0], 1, row_tab[...], col_tab[1])
     store = pltpu.make_async_copy(spec, spec_out, local_sems.at[0])
     store.start()
 
@@ -393,27 +399,28 @@
         window = window_at(
             small32, off_row + COARSE, off_col + LANES, small_rows, small_cols
         )
-        other = forward(
-            normalized(window, 1.0 / math.sqrt(small_rows * small_cols)), row_tab[...], col_tab[1]
-        )
+        flat = normalized([window], [1.0 / math.sqrt(small_rows * small_cols)])[0]
+        other = forward(flat, 1, row_tab[...], col_tab[1])
         product = multiply(spec[pl.num_programs(0) * pairs], other, LANES)
-        coarse_out[0] = inverse_cols(inverse_rows(product, inv_row[...]), inv_col[1])
-
+        coarse_out[0] = inverse([product], 1, inv_row[...], inv_col[1])
+
+    windows = []
+    scales = []
+    for column in range(2 * pairs):
+        row_at = HALO + band * P_SIZE + DS * off_row + peaks[0, band, 0, column]
+        col_at = LANES + column * P_SIZE + DS * off_col + peaks[0, band, 1, column]
+        windows.append(window_at(ext32, row_at, col_at, P_SIZE, P_SIZE))
+        scales.append(keep[0, band, column].astype(jnp.float32) * (1.0 / P_SIZE))
+    flat = normalized(windows, scales)
+    stack = along(jnp.concatenate(flat, axis=1), pairs)
+    spectra = forward(stack, pairs, row_tab[...], col_tab[0])
+    products = [
+        multiply(spec[band * pairs + j], spectra[:, j * PAIR : (j + 1) * PAIR], P_SIZE // 2)
+        for j in range(pairs)
+    ]
+    maps = inverse(products, pairs, inv_row[...], inv_col[0])
     for j in range(pairs):
-        halves = []
-        for n in range(2):
-            column = 2 * j + n
-            row_at = HALO + band * P_SIZE + DS * off_row + peaks[0, band, 0, column]
-            col_at = LANES + column * P_SIZE + DS * off_col + peaks[0, band, 1, column]
-            window = window_at(ext32, row_at, col_at, P_SIZE, P_SIZE)
-            halves.append(
-                normalized(window, keep[0, band, column].astype(jnp.float32) * (1.0 / P_SIZE))
-            )
-        other = forward(jnp.concatenate(halves, axis=1), row_tab[...], col_tab[0])
-        product = multiply(spec[band * pairs + j], other, P_SIZE // 2)
-        flow_out[0, :, j * PAIR : (j + 1) * PAIR] = inverse_cols(
-            inverse_rows(product, inv_row[...]), inv_col[0]
-        )
+        flow_out[0, :, j * PAIR : (j + 1) * PAIR] = maps[j * P_SIZE : (j + 1) * P_SIZE]
 
 
 def shards(nt, section_image, offsets, peak_shift, accepted):

time: 31.6 us -> 27.5 us (0.87)
  Pallas kernels: 30.8 us -> 26.7 us
    pallas_call x1, Pallas kernels: 15.1 us -> 11 us  [shards(): pl.pallas_call(functools.partial(match_kernel, pairs, nt), name='match',...]
where the time goes in v2:
time: 27.5 us; the launch traced here: 27.3 us
  Pallas kernels  26.7 us (97%)
  between operations  0.64 us (2%)
    pallas_call x1, Pallas kernels, shards(): pl.pallas_call(functools.partial(exchange_kernel, chunks, bands, pairs),...  15.7 us
    pallas_call x1, Pallas kernels, shards(): pl.pallas_call(functools.partial(match_kernel, pairs, nt), name='match',...  11 us

profile of v2, /device:TPU:20, one launch (start us, length us, event | category | flops | bytes accessed | tf_op | source)
XLA Modules:
  0.0 27.3 jit_solution(13777512917677794038)
XLA Ops:
  0.6 15.7 %exchange.1 = (bf16[672,1024]{1,0:T(8,128)(2,1)}, f32[17,128,256]{2,1,0:T(8,128)}) custom-call(bf16[512,1024]{1,0:T(8,128)(2,1)} %bitcast.2, bf16[128,256]{1,0:T(8,128)(2,1)} %constant.10.clone.row_hbm.row_tab, bf16[2,512,256]{2,1,0:T(8,128)(2,1)} %constant.12.clone.col_hbm.col_tab, bf16[512,128]{1,0:T(8,128)(2,1)} %constant.14.clone.pool_hbm.pool), custom_call_target="tpu_custom_call" | custom-call | tf_op jit(solution)/shard_map/exchange/pallas_call | solution.py:437
  16.3 11.0 %match.1 = (f32[1,128,256]{2,1,0:T(8,128)}, f32[1,512,1024]{2,1,0:T(8,128)}) custom-call(s32[1,1,2]{2,1,0:T(1,128)} %offsets.1, s32[1,4,2,8]{3,2,1,0:T(2,128)} %bitcast.3, s32[1,4,8]{2,1,0:T(4,128)} %keep.1, bf16[672,1024]{1,0:T(8,128)(2,1)} %get-tuple-element.4.ext, f32[17,128,256]{2,1,0:T(8,128)} %get-tuple-element.5.spec, ...), custom_call_target="tpu_custom_call" | custom-call | tf_op jit(solution)/shard_map/match/pallas_call | solution.py:464

commit v3 on v2

--- a/solution.py
+++ b/solution.py
@@ -344,6 +344,7 @@
     keep,
     ext,
     spec,
+    coarse_spec,
     row_tab,
     col_tab,
     inv_row,
@@ -401,7 +402,7 @@
         )
         flat = normalized([window], [1.0 / math.sqrt(small_rows * small_cols)])[0]
         other = forward(flat, 1, row_tab[...], col_tab[1])
-        product = multiply(spec[pl.num_programs(0) * pairs], other, LANES)
+        product = multiply(coarse_spec[0], other, LANES)
         coarse_out[0] = inverse([product], 1, inv_row[...], inv_col[1])
 
     windows = []
@@ -415,7 +416,7 @@
     stack = along(jnp.concatenate(flat, axis=1), pairs)
     spectra = forward(stack, pairs, row_tab[...], col_tab[0])
     products = [
-        multiply(spec[band * pairs + j], spectra[:, j * PAIR : (j + 1) * PAIR], P_SIZE // 2)
+        multiply(spec[j], spectra[:, j * PAIR : (j + 1) * PAIR], P_SIZE // 2)
         for j in range(pairs)
     ]
     maps = inverse(products, pairs, inv_row[...], inv_col[0])
@@ -469,10 +470,19 @@
             jax.ShapeDtypeStruct((1, rows // DS, width // DS), jnp.float32),
             jax.ShapeDtypeStruct((1, rows, width), jnp.float32),
         ),
-        in_specs=[smem, smem, smem]
+        in_specs=[
+            smem,
+            smem,
+            smem,
+            whole(ext.shape),
+            pl.BlockSpec((pairs, P_SIZE, PAIR), lambda i: (i, 0, 0)),
+            pl.BlockSpec(
+                (1, P_SIZE, PAIR), lambda i: (units - 1, 0, 0), pipeline_mode=pl.Buffered(1)
+            ),
+        ]
         + [
             whole(x.shape)
-            for x in (ext, spec, forward_row, forward_col, inverse_row, inverse_col, pool)
+            for x in (forward_row, forward_col, inverse_row, inverse_col, pool)
         ],
         out_specs=(
             pl.BlockSpec((1, rows // DS, width // DS), lambda i: (0, 0, 0)),
@@ -483,7 +493,7 @@
             pltpu.VMEM((rows // DS + 2 * COARSE + SUB, width // DS + 2 * LANES), jnp.float32),
         ],
         compiler_params=pltpu.CompilerParams(dimension_semantics=("arbitrary",)),
-    )(offsets, jnp.swapaxes(peak_shift, 2, 3), accepted, ext, spec, forward_row, forward_col, inverse_row, inverse_col, pool)
+    )(offsets, jnp.swapaxes(peak_shift, 2, 3), accepted, ext, spec, spec, forward_row, forward_col, inverse_row, inverse_col, pool)
     return coarse_map, flow_map
 
 

time: 27.5 us -> 27 us (0.982)
  Pallas kernels: 26.7 us -> 26.2 us
    pallas_call x1, Pallas kernels: 11 us -> 10.6 us  [shards(): pl.pallas_call(functools.partial(match_kernel, pairs, nt), name='match',...]
where the time goes in v3:
time: 27 us; the launch traced here: 26.9 us
  Pallas kernels  26.2 us (97%)
  between operations  0.64 us (2%)
    pallas_call x1, Pallas kernels, shards(): pl.pallas_call(functools.partial(exchange_kernel, chunks, bands, pairs),...  15.7 us
    pallas_call x1, Pallas kernels, shards(): pl.pallas_call(functools.partial(match_kernel, pairs, nt), name='match',...  10.6 us

profile of v3, /device:TPU:20, one launch (start us, length us, event | category | flops | bytes accessed | tf_op | source)
XLA Modules:
  0.0 26.9 jit_solution(15523399848951604299)
XLA Ops:
  0.6 15.7 %exchange.1 = (bf16[672,1024]{1,0:T(8,128)(2,1)}, f32[17,128,256]{2,1,0:T(8,128)}) custom-call(bf16[512,1024]{1,0:T(8,128)(2,1)} %bitcast.2, bf16[128,256]{1,0:T(8,128)(2,1)} %constant.10.clone.row_hbm.row_tab, bf16[2,512,256]{2,1,0:T(8,128)(2,1)} %constant.12.clone.col_hbm.col_tab, bf16[512,128]{1,0:T(8,128)(2,1)} %constant.14.clone.pool_hbm.pool), custom_call_target="tpu_custom_call" | custom-call | tf_op jit(solution)/shard_map/exchange/pallas_call | solution.py:438
  16.3 10.6 %match.1 = (f32[1,128,256]{2,1,0:T(8,128)}, f32[1,512,1024]{2,1,0:T(8,128)}) custom-call(s32[1,1,2]{2,1,0:T(1,128)} %offsets.1, s32[1,4,2,8]{3,2,1,0:T(2,128)} %bitcast.3, s32[1,4,8]{2,1,0:T(4,128)} %keep.1, bf16[672,1024]{1,0:T(8,128)(2,1)} %get-tuple-element.4.ext, f32[17,128,256]{2,1,0:T(8,128)} %get-tuple-element.5.spec.coarse_spec, ...), custom_call_target="tpu_custom_call" | custom-call | tf_op jit(solution)/shard_map/match/pallas_call | solution.py:465

commit v4 on v3

--- a/solution.py
+++ b/solution.py
@@ -442,7 +442,7 @@
             jax.ShapeDtypeStruct((rows + 2 * HALO, width), jnp.bfloat16),
             jax.ShapeDtypeStruct((units, P_SIZE, PAIR), jnp.float32),
         ),
-        in_specs=[hbm] * 4,
+        in_specs=[pl.BlockSpec(memory_space=pltpu.HBM)] * 4,
         out_specs=(hbm, hbm),
         scratch_shapes=[
             pltpu.VMEM((rows, width), jnp.bfloat16),
@@ -454,7 +454,9 @@
             pltpu.SemaphoreType.DMA((len(chunks) + 2,)),
             pltpu.SemaphoreType.DMA((4,)),
         ],
-        compiler_params=pltpu.CompilerParams(collective_id=0, has_side_effects=True),
+        compiler_params=pltpu.CompilerParams(
+            collective_id=0, has_side_effects=True, vmem_limit_bytes=16 * 2**20
+        ),
     )(own, forward_row, forward_col, pool)
 
     def whole(shape):
@@ -492,7 +494,9 @@
             pltpu.VMEM((rows + 2 * HALO + SUB, width + 2 * LANES), jnp.float32),
             pltpu.VMEM((rows // DS + 2 * COARSE + SUB, width // DS + 2 * LANES), jnp.float32),
         ],
-        compiler_params=pltpu.CompilerParams(dimension_semantics=("arbitrary",)),
+        compiler_params=pltpu.CompilerParams(
+            dimension_semantics=("arbitrary",), vmem_limit_bytes=24 * 2**20
+        ),
     )(offsets, jnp.swapaxes(peak_shift, 2, 3), accepted, ext, spec, spec, forward_row, forward_col, inverse_row, inverse_col, pool)
     return coarse_map, flow_map
 

time: 27 us -> 33.7 us (1.25)
  local copies, waits for them, and re-layouts: 0 us -> 7.71 us
  Pallas kernels: 26.2 us -> 24.9 us
    unnamed x0 -> x22, local copies, waits for them, and re-layouts: none -> 7.71 us
    pallas_call x1, Pallas kernels: 10.6 us -> 9.2 us  [shards(): pl.pallas_call(functools.partial(match_kernel, pairs, nt), name='match',...]
where the time goes in v4:
time: 33.7 us; the launch traced here: 33.3 us
  Pallas kernels  24.9 us (74%)
  local copies, waits for them, and re-layouts  7.71 us (23%)
  between operations  0.68 us (2%)
    pallas_call x1, Pallas kernels, shards(): pl.pallas_call(functools.partial(exchange_kernel, chunks, bands, pairs),...  15.7 us
    pallas_call x1, Pallas kernels, shards(): pl.pallas_call(functools.partial(match_kernel, pairs, nt), name='match',...  9.2 us
    unnamed x22, local copies, waits for them, and re-layouts  7.71 us

profile of v4, /device:TPU:20, one launch (start us, length us, event | category | flops | bytes accessed | tf_op | source)
XLA Modules:
  0.0 33.3 jit_solution(1567366045672386912)
XLA Ops:
  0.6 0.0 copy-start
  0.6 1.0 %copy-done = bf16[2,512,256]{2,1,0:T(8,128)(2,1)S(1)} copy-done((bf16[2,512,256]{2,1,0:T(8,128)(2,1)S(1)}, bf16[2,512,256]{2,1,0:T(8,128)(2,1)}, u32[]{:S(2)}) %copy-start) | copy-done | bytes 524312
  1.7 0.0 copy-start.2
  1.7 1.2 %copy-done.2 = bf16[1,512,1024]{2,1,0:T(8,128)(2,1)S(1)} copy-done((bf16[1,512,1024]{2,1,0:T(8,128)(2,1)S(1)}, bf16[1,512,1024]{2,1,0:T(8,128)(2,1)}, u32[]{:S(2)}) %copy-start.2) | copy-done | bytes 1048600
  2.9 0.0 copy-start.4
  2.9 0.9 %copy-done.4 = bf16[512,128]{1,0:T(8,128)(2,1)S(1)} copy-done((bf16[512,128]{1,0:T(8,128)(2,1)S(1)}, bf16[512,128]{1,0:T(8,128)(2,1)}, u32[]{:S(2)}) %copy-start.4) | copy-done | bytes 131096
  3.8 0.0 copy-start.5
  3.8 0.8 %copy-done.5 = bf16[128,256]{1,0:T(8,128)(2,1)S(1)} copy-done((bf16[128,256]{1,0:T(8,128)(2,1)S(1)}, bf16[128,256]{1,0:T(8,128)(2,1)}, u32[]{:S(2)}) %copy-start.5) | copy-done | bytes 65560
  4.6 0.0 copy-start.1
  4.6 0.0 copy-start.3
  4.6 15.7 %exchange.1 = (bf16[672,1024]{1,0:T(8,128)(2,1)S(1)}, f32[17,128,256]{2,1,0:T(8,128)S(1)}) custom-call(bf16[512,1024]{1,0:T(8,128)(2,1)S(1)} %bitcast.2, bf16[128,256]{1,0:T(8,128)(2,1)S(1)} %copy-done.5, bf16[2,512,256]{2,1,0:T(8,128)(2,1)S(1)} %copy-done, bf16[512,128]{1,0:T(8,128)(2,1)S(1)} %copy-done.4), custom_call_target="tpu_custom_call" | custom-call | tf_op jit(solution)/shard_map/exchange/pallas_call | solution.py:438
  20.3 0.0 copy-done.1
  20.3 0.0 copy-done.3
  20.3 0.0 copy-start.6
  20.4 0.8 %copy-done.6 = bf16[128,256]{1,0:T(8,128)(2,1)S(1)} copy-done((bf16[128,256]{1,0:T(8,128)(2,1)S(1)}, bf16[128,256]{1,0:T(8,128)(2,1)}, u32[]{:S(2)}) %copy-start.6) | copy-done | bytes 65560
  21.2 0.0 copy-start.7
  21.2 0.8 %copy-done.7 = bf16[128,256]{1,0:T(8,128)(2,1)S(1)} copy-done((bf16[128,256]{1,0:T(8,128)(2,1)S(1)}, bf16[128,256]{1,0:T(8,128)(2,1)}, u32[]{:S(2)}) %copy-start.7) | copy-done | bytes 65560
  22.0 0.0 copy-start.8
  22.0 0.7 %copy-done.8 = s32[1,4,8,2]{2,3,1,0:T(2,128)S(1)} copy-done((s32[1,4,8,2]{2,3,1,0:T(2,128)S(1)}, s32[1,4,8,2]{2,3,1,0:T(2,128)}, u32[]{:S(2)}) %copy-start.8) | copy-done | bytes 280
  22.7 0.0 copy-start.9
  22.7 0.7 %copy-done.9 = s32[1,4,8]{2,1,0:T(4,128)S(1)} copy-done((s32[1,4,8]{2,1,0:T(4,128)S(1)}, s32[1,4,8]{2,1,0:T(4,128)}, u32[]{:S(2)}) %copy-start.9) | copy-done | bytes 152
  23.4 0.0 copy-start.10
  23.4 0.7 %copy-done.10 = s32[1,1,2]{2,1,0:T(1,128)S(1)} copy-done((s32[1,1,2]{2,1,0:T(1,128)S(1)}, s32[1,1,2]{2,1,0:T(1,128)}, u32[]{:S(2)}) %copy-start.10) | copy-done | bytes 32
  24.1 9.2 %match.1 = (f32[1,128,256]{2,1,0:T(8,128)}, f32[1,512,1024]{2,1,0:T(8,128)}) custom-call(s32[1,1,2]{2,1,0:T(1,128)S(1)} %copy-done.10, s32[1,4,2,8]{3,2,1,0:T(2,128)S(1)} %bitcast.3, s32[1,4,8]{2,1,0:T(4,128)S(1)} %copy-done.9, bf16[672,1024]{1,0:T(8,128)(2,1)S(1)} %get-tuple-element.4.ext, f32[17,128,256]{2,1,0:T(8,128)S(1)} %get-tuple-element.5.spec.coarse_spec, ...), custom_call_target="tpu_custom_call" | custom-call | tf_op jit(solution)/shard_map/match/pallas_call | solution.py:467
Async XLA Ops:
  0.6 1.0 %copy-start = (bf16[2,512,256]{2,1,0:T(8,128)(2,1)S(1)}, bf16[2,512,256]{2,1,0:T(8,128)(2,1)}, u32[]{:S(2)}) copy-start(bf16[2,512,256]{2,1,0:T(8,128)(2,1)} %constant.12.clone.col_hbm.col_tab) | copy-start | bytes 1572868
  1.7 1.2 %copy-start.2 = (bf16[1,512,1024]{2,1,0:T(8,128)(2,1)S(1)}, bf16[1,512,1024]{2,1,0:T(8,128)(2,1)}, u32[]{:S(2)}) copy-start(bf16[1,512,1024]{2,1,0:T(8,128)(2,1)} %param.9) | copy-start | bytes 3145732
  2.9 0.9 %copy-start.4 = (bf16[512,128]{1,0:T(8,128)(2,1)S(1)}, bf16[512,128]{1,0:T(8,128)(2,1)}, u32[]{:S(2)}) copy-start(bf16[512,128]{1,0:T(8,128)(2,1)} %constant.14.clone.pool_hbm.pool) | copy-start | bytes 393220
  3.8 0.8 %copy-start.5 = (bf16[128,256]{1,0:T(8,128)(2,1)S(1)}, bf16[128,256]{1,0:T(8,128)(2,1)}, u32[]{:S(2)}) copy-start(bf16[128,256]{1,0:T(8,128)(2,1)} %constant.10.clone.row_hbm.row_tab) | copy-start | bytes 196612
  4.6 15.7 %copy-start.1 = (bf16[2,512,256]{2,1,0:T(8,128)(2,1)S(1)}, bf16[2,512,256]{2,1,0:T(8,128)(2,1)}, u32[]{:S(2)}) copy-start(bf16[2,512,256]{2,1,0:T(8,128)(2,1)} %constant.12.clone.col_hbm.col_tab) | copy-start | bytes 1572868
  4.6 15.7 %copy-start.3 = (bf16[2,512,256]{2,1,0:T(8,128)(2,1)S(1)}, bf16[2,512,256]{2,1,0:T(8,128)(2,1)}, u32[]{:S(2)}) copy-start(bf16[2,512,256]{2,1,0:T(8,128)(2,1)} %constant.13.clone.inv_col) | copy-start | bytes 1572868
  20.3 0.8 %copy-start.6 = (bf16[128,256]{1,0:T(8,128)(2,1)S(1)}, bf16[128,256]{1,0:T(8,128)(2,1)}, u32[]{:S(2)}) copy-start(bf16[128,256]{1,0:T(8,128)(2,1)} %constant.10.clone.row_hbm.row_tab) | copy-start | bytes 196612
  21.2 0.8 %copy-start.7 = (bf16[128,256]{1,0:T(8,128)(2,1)S(1)}, bf16[128,256]{1,0:T(8,128)(2,1)}, u32[]{:S(2)}) copy-start(bf16[128,256]{1,0:T(8,128)(2,1)} %constant.11.clone.inv_row) | copy-start | bytes 196612
  22.0 0.7 %copy-start.8 = (s32[1,4,8,2]{2,3,1,0:T(2,128)S(1)}, s32[1,4,8,2]{2,3,1,0:T(2,128)}, u32[]{:S(2)}) copy-start(s32[1,4,8,2]{2,3,1,0:T(2,128)} %param.11) | copy-start | bytes 772
  22.7 0.7 %copy-start.9 = (s32[1,4,8]{2,1,0:T(4,128)S(1)}, s32[1,4,8]{2,1,0:T(4,128)}, u32[]{:S(2)}) copy-start(s32[1,4,8]{2,1,0:T(4,128)} %keep.1) | copy-start | bytes 388
  23.4 0.7 %copy-start.10 = (s32[1,1,2]{2,1,0:T(1,128)S(1)}, s32[1,1,2]{2,1,0:T(1,128)}, u32[]{:S(2)}) copy-start(s32[1,1,2]{2,1,0:T(1,128)} %offsets.1) | copy-start | bytes 28

commit v5 on v3

--- a/solution.py
+++ b/solution.py
@@ -405,23 +405,29 @@
         product = multiply(coarse_spec[0], other, LANES)
         coarse_out[0] = inverse([product], 1, inv_row[...], inv_col[1])
 
+    per = flow_out.shape[1] // P_SIZE
     windows = []
     scales = []
-    for column in range(2 * pairs):
-        row_at = HALO + band * P_SIZE + DS * off_row + peaks[0, band, 0, column]
-        col_at = LANES + column * P_SIZE + DS * off_col + peaks[0, band, 1, column]
-        windows.append(window_at(ext32, row_at, col_at, P_SIZE, P_SIZE))
-        scales.append(keep[0, band, column].astype(jnp.float32) * (1.0 / P_SIZE))
+    for r in range(per):
+        for column in range(2 * pairs):
+            row = band * per + r
+            row_at = HALO + row * P_SIZE + DS * off_row + peaks[0, row, 0, column]
+            col_at = LANES + column * P_SIZE + DS * off_col + peaks[0, row, 1, column]
+            windows.append(window_at(ext32, row_at, col_at, P_SIZE, P_SIZE))
+            scales.append(keep[0, row, column].astype(jnp.float32) * (1.0 / P_SIZE))
     flat = normalized(windows, scales)
-    stack = along(jnp.concatenate(flat, axis=1), pairs)
-    spectra = forward(stack, pairs, row_tab[...], col_tab[0])
+    count = per * pairs
+    stack = along(jnp.concatenate(flat, axis=1), count)
+    spectra = forward(stack, count, row_tab[...], col_tab[0])
     products = [
-        multiply(spec[j], spectra[:, j * PAIR : (j + 1) * PAIR], P_SIZE // 2)
-        for j in range(pairs)
+        multiply(spec[j], spectra[:, j * PAIR : (j + 1) * PAIR], P_SIZE // 2) for j in range(count)
     ]
-    maps = inverse(products, pairs, inv_row[...], inv_col[0])
-    for j in range(pairs):
-        flow_out[0, :, j * PAIR : (j + 1) * PAIR] = maps[j * P_SIZE : (j + 1) * P_SIZE]
+    maps = inverse(products, count, inv_row[...], inv_col[0])
+    for n in range(count):
+        r, j = divmod(n, pairs)
+        flow_out[0, r * P_SIZE : (r + 1) * P_SIZE, j * PAIR : (j + 1) * PAIR] = maps[
+            n * P_SIZE : (n + 1) * P_SIZE
+        ]
 
 
 def shards(nt, section_image, offsets, peak_shift, accepted):
@@ -435,6 +441,7 @@
     vmem = pl.BlockSpec(memory_space=pltpu.VMEM)
     smem = pl.BlockSpec(memory_space=pltpu.SMEM)
     units = bands * pairs + 1
+    per = 2 if bands % 2 == 0 else 1
     ext, spec = pl.pallas_call(
         functools.partial(exchange_kernel, chunks, bands, pairs),
         name="exchange",
@@ -465,7 +472,7 @@
     coarse_map, flow_map = pl.pallas_call(
         functools.partial(match_kernel, pairs, nt),
         name="match",
-        grid=(bands,),
+        grid=(bands // per,),
         out_shape=(
             jax.ShapeDtypeStruct((1, rows // DS, width // DS), jnp.float32),
             jax.ShapeDtypeStruct((1, rows, width), jnp.float32),
@@ -475,7 +482,7 @@
             smem,
             smem,
             whole(ext.shape),
-            pl.BlockSpec((pairs, P_SIZE, PAIR), lambda i: (i, 0, 0)),
+            pl.BlockSpec((per * pairs, P_SIZE, PAIR), lambda i: (i, 0, 0)),
             pl.BlockSpec(
                 (1, P_SIZE, PAIR), lambda i: (units - 1, 0, 0), pipeline_mode=pl.Buffered(1)
             ),
@@ -486,7 +493,7 @@
         ],
         out_specs=(
             pl.BlockSpec((1, rows // DS, width // DS), lambda i: (0, 0, 0)),
-            pl.BlockSpec((1, P_SIZE, width), lambda i: (0, i, 0)),
+            pl.BlockSpec((1, per * P_SIZE, width), lambda i: (0, i, 0)),
         ),
         scratch_shapes=[
             pltpu.VMEM((rows + 2 * HALO + SUB, width + 2 * LANES), jnp.float32),

time: 27 us -> 26 us (0.963)
  Pallas kernels: 26.2 us -> 25.2 us
    pallas_call x1, Pallas kernels: 10.6 us -> 9.5 us  [shards(): pl.pallas_call(functools.partial(match_kernel, pairs, nt), name='match',...]
where the time goes in v5:
time: 26 us; the launch traced here: 25.8 us
  Pallas kernels  25.2 us (97%)
  between operations  0.64 us (2%)
    pallas_call x1, Pallas kernels, shards(): pl.pallas_call(functools.partial(exchange_kernel, chunks, bands, pairs),...  15.7 us
    pallas_call x1, Pallas kernels, shards(): pl.pallas_call(functools.partial(match_kernel, pairs, nt), name='match',...  9.5 us

profile of v5, /device:TPU:20, one launch (start us, length us, event | category | flops | bytes accessed | tf_op | source)
XLA Modules:
  0.0 25.8 jit_solution(10369079724457328180)
XLA Ops:
  0.6 15.7 %exchange.1 = (bf16[672,1024]{1,0:T(8,128)(2,1)}, f32[17,128,256]{2,1,0:T(8,128)}) custom-call(bf16[512,1024]{1,0:T(8,128)(2,1)} %bitcast.2, bf16[128,256]{1,0:T(8,128)(2,1)} %constant.10.clone.row_hbm.row_tab, bf16[2,512,256]{2,1,0:T(8,128)(2,1)} %constant.12.clone.col_hbm.col_tab, bf16[512,128]{1,0:T(8,128)(2,1)} %constant.14.clone.pool_hbm.pool), custom_call_target="tpu_custom_call" | custom-call | tf_op jit(solution)/shard_map/exchange/pallas_call | solution.py:445
  16.3 9.5 %match.1 = (f32[1,128,256]{2,1,0:T(8,128)}, f32[1,512,1024]{2,1,0:T(8,128)}) custom-call(s32[1,1,2]{2,1,0:T(1,128)} %offsets.1, s32[1,4,2,8]{3,2,1,0:T(2,128)} %bitcast.3, s32[1,4,8]{2,1,0:T(4,128)} %keep.1, bf16[672,1024]{1,0:T(8,128)(2,1)} %get-tuple-element.4.ext, f32[17,128,256]{2,1,0:T(8,128)} %get-tuple-element.5.spec.coarse_spec, ...), custom_call_target="tpu_custom_call" | custom-call | tf_op jit(solution)/shard_map/match/pallas_call | solution.py:472
